TPU v7x, 32 devices: a whole 2x2x4 slice. The times are simulated.
32 devices in a mesh: seq: 2 (over x), batch: 4 (over y, core), head: 4 (over z).
Axes of the slice: x: 2, y: 2, z: 4, core: 2. Of those that a mesh axis runs over, the one named last changes fastest.
Arguments:
- hidden: bfloat16 [4, 256, 16384], P('batch', None, 'seq'), may hold values from -760 to 760
- gain: float32 [16384], P('seq'), may hold values from 0.5 to 1.5
- key_weight: bfloat16 [16384, 1024], P('seq', 'head'), may hold values from -0.046875 to 0.046875
- value_weight: bfloat16 [16384, 1024], P('seq', 'head'), may hold values from -0.046875 to 0.046875
- positions: int32 [4, 256], P('batch', 'seq'), may hold values from 0 to 32767
- initial_basis: float32 [2048, 256], P('head'), may hold values from -6 to 6
Outputs:
- basis: float32 [2048, 256], P('head')
All inputs are finite; a program needn't handle non-finite values.
Results may differ from a plain program's by a relative error of at most 0.0063.
Values may be sent and summed in bfloat16 or wider, within the bound.
A program may use at most 64 MiB of HBM per device.

v0:
```python
import math
import jax
import jax.numpy as jnp
from jax import lax
from jax.sharding import PartitionSpec as P

D = 16384
HEAD_DIM = 128
ITERS = 4
EPSILON = 1e-05
ROTARY_BASE = 500000.0


def rotary(head_rows, position_row):
    half_width = head_rows.shape[-1] // 2
    index_row = jnp.arange(half_width, dtype=jnp.float32)
    frequency = jnp.exp(index_row * (-math.log(ROTARY_BASE) / half_width))
    angles = position_row.astype(jnp.float32)[:, None] * frequency[None, :]
    cosine = jnp.cos(angles)[:, None, :]
    sine_part = jnp.sin(angles)[:, None, :]
    first_half = head_rows[..., :half_width]
    second_half = head_rows[..., half_width:]
    return jnp.concatenate(
        [
            first_half * cosine - second_half * sine_part,
            second_half * cosine + first_half * sine_part,
        ],
        axis=-1,
    )


def whole_of(basis_block):
    return lax.all_gather(basis_block, "head", axis=0, tiled=True)


def total_squares(local_squares, local_tokens):
    all_squares = lax.psum(local_squares, "seq")
    return lax.dynamic_slice_in_dim(all_squares, lax.axis_index("seq") * local_tokens, local_tokens)


def gram_of(images):
    return lax.dot_general(
        images,
        images,
        (((0,), (0,)), ((), ())),
        precision=lax.Precision.HIGHEST,
        preferred_element_type=jnp.float32,
    )


def orthonormal(images, gram_matrix):
    factor = jnp.linalg.cholesky(gram_matrix)
    return lax.linalg.triangular_solve(
        factor, images, left_side=False, lower=True, transpose_a=True
    )


def body(hidden, gain, key_weight, value_weight, positions, initial_basis):
    hidden_rows = hidden[0]
    local_tokens = positions.shape[1]
    widened = hidden_rows.astype(jnp.float32)
    scaled = (widened * gain).astype(jnp.bfloat16)
    local_squares = jnp.sum(widened * widened, axis=1)
    key_columns = key_weight.shape[1]
    weights = jnp.concatenate([key_weight, value_weight], axis=1)
    own_squares = total_squares(local_squares, local_tokens)
    projected = lax.psum_scatter(
        jnp.dot(scaled, weights, preferred_element_type=jnp.float32),
        "seq",
        scatter_dimension=0,
        tiled=True,
    )
    inverse_scale = lax.rsqrt(own_squares / D + EPSILON)
    projected = projected * inverse_scale[:, None]
    key_rows = rotary(projected[:, :key_columns].reshape(local_tokens, -1, HEAD_DIM), positions[0])
    value_rows = projected[:, key_columns:].reshape(local_tokens, -1, HEAD_DIM)
    joint_rows = (
        jnp.stack([key_rows, value_rows], axis=2).reshape(local_tokens, -1).astype(jnp.bfloat16)
    )
    partial_value = lax.dot_general(
        joint_rows,
        lax.all_gather(joint_rows, "head", axis=1, tiled=True),
        (((0,), (0,)), ((), ())),
        preferred_element_type=jnp.float32,
    )
    token_total = local_tokens * lax.axis_size("seq") * lax.axis_size("batch")
    basis_block = initial_basis
    covariance = lax.psum(partial_value, ("seq", "batch")) / token_total
    for iteration in range(ITERS):
        whole_basis = whole_of(basis_block)
        images = jnp.dot(
            covariance,
            whole_basis,
            precision=lax.Precision.HIGHEST,
            preferred_element_type=jnp.float32,
        )
        gram_matrix = lax.psum(gram_of(images), "head") / whole_basis.shape[0]
        basis_block = orthonormal(images, gram_matrix)
    return basis_block


def solution(mesh):
    return jax.shard_map(
        body,
        mesh=mesh,
        in_specs=(
            P("batch", None, "seq"),
            P("seq"),
            P("seq", "head"),
            P("seq", "head"),
            P("batch", "seq"),
            P("head", None),
        ),
        out_specs=P("head", None),
        check_vma=False,
    )
```

profile of v0, /device:TPU:0, one launch (start us, length us, event | category | flops | bytes accessed | tf_op | source)
XLA Modules:
  0.0 718.3 jit_solution(16877559719014018275)
XLA Ops:
  34.1 15.5 %all_gather.15 = bf16[128,2048]{0,1:T(8,128)(2,1)S(1)} all-gather(bf16[128,512]{0,1:T(8,128)(2,1)S(1)} %bitcast.160), channel_id=1, replica_groups=mesh['seq'=2,'batch'=4,'head'=4] {'head'}, dimensions={1}, use_global_device_ids=true | all-gather | bytes 655360 | tf_op jit(solution)/shard_map/all_gather | solution.py:82
  52.9 81.2 %all-reduce.7.cloned.1.call-done = f32[512,2048]{1,0:T(8,128)} async-done(((f32[512,2048]{1,0:T(8,128)}), f32[512,2048]{1,0:T(8,128)}) %all-reduce.7.cloned.1.call-update) | async-done | bytes 4194320 | tf_op jit(solution)/shard_map/psum | solution.py:88
  142.3 35.4 %all-reduce.9.cloned.1.call-done = f32[256,256]{0,1:T(8,128)} async-done(((f32[256,256]{0,1:T(8,128)}), f32[256,256]{0,1:T(8,128)}) %all-reduce.9.cloned.1.call-update) | async-done | bytes 262160 | tf_op jit(solution)/shard_map/psum | solution.py:97
  179.8 11.7 %cholesky.214 = f32[128,128]{1,0:T(8,128)S(1)} custom-call(f32[128,128]{1,0:T(8,128)S(1)} %cholesky.346), custom_call_target="Cholesky" | custom-call | tf_op jit(solution)/shard_map/jit(cholesky)/cholesky | solution.py:52
  191.5 9.8 %custom-call.17 = f32[1,128,128]{1,2,0:T(8,128)S(1)} custom-call(f32[1,128,128]{2,1,0:T(8,128)S(1)} %get-tuple-element.94), custom_call_target="InvertDiagBlocksLowerTriangular" | custom-call | tf_op jit(solution)/shard_map/jit(cholesky)/cholesky | solution.py:52
  201.8 11.7 %cholesky.231 = f32[128,128]{1,0:T(8,128)S(1)} custom-call(f32[128,128]{1,0:T(8,128)S(1)} %convolution_subtract_fusion.7), custom_call_target="Cholesky" | custom-call | tf_op jit(solution)/shard_map/jit(cholesky)/cholesky | solution.py:52
  220.1 19.7 %custom-call.18 = f32[2,128,128]{1,2,0:T(8,128)S(1)} custom-call(f32[2,128,128]{2,1,0:T(8,128)S(1)} %get-tuple-element.33), custom_call_target="InvertDiagBlocksLowerTriangular" | custom-call | tf_op jit(solution)/shard_map/triangular_solve/custom-call.0 | solution.py:53
  242.1 45.1 %all-gather.7.cloned.1.call-done = f32[2048,256]{0,1:T(8,128)} async-done(((f32[512,256]{0,1:T(8,128)}), f32[2048,256]{0,1:T(8,128)}) %all-gather.7.cloned.1.call-update) | async-done | bytes 2097168 | tf_op jit(solution)/shard_map/all_gather | solution.py:33
  295.3 34.3 %all-reduce.11.cloned.1.call-done = f32[256,256]{0,1:T(8,128)} async-done(((f32[256,256]{0,1:T(8,128)}), f32[256,256]{0,1:T(8,128)}) %all-reduce.11.cloned.1.call-update) | async-done | bytes 262160 | tf_op jit(solution)/shard_map/psum | solution.py:97
  331.6 11.7 %cholesky.248 = f32[128,128]{1,0:T(8,128)S(1)} custom-call(f32[128,128]{1,0:T(8,128)S(1)} %cholesky.349), custom_call_target="Cholesky" | custom-call | tf_op jit(solution)/shard_map/jit(cholesky)/cholesky | solution.py:52
  343.4 9.8 %custom-call.19 = f32[1,128,128]{1,2,0:T(8,128)S(1)} custom-call(f32[1,128,128]{2,1,0:T(8,128)S(1)} %get-tuple-element.90), custom_call_target="InvertDiagBlocksLowerTriangular" | custom-call | tf_op jit(solution)/shard_map/jit(cholesky)/cholesky | solution.py:52
  353.7 11.7 %cholesky.265 = f32[128,128]{1,0:T(8,128)S(1)} custom-call(f32[128,128]{1,0:T(8,128)S(1)} %convolution_subtract_fusion.6), custom_call_target="Cholesky" | custom-call | tf_op jit(solution)/shard_map/jit(cholesky)/cholesky | solution.py:52
  372.2 19.7 %custom-call.20 = f32[2,128,128]{1,2,0:T(8,128)S(1)} custom-call(f32[2,128,128]{2,1,0:T(8,128)S(1)} %get-tuple-element.34), custom_call_target="InvertDiagBlocksLowerTriangular" | custom-call | tf_op jit(solution)/shard_map/triangular_solve/custom-call.0 | solution.py:53
  394.3 45.1 %all-gather.9.cloned.1.call-done = f32[2048,256]{0,1:T(8,128)} async-done(((f32[512,256]{0,1:T(8,128)}), f32[2048,256]{0,1:T(8,128)}) %all-gather.9.cloned.1.call-update) | async-done | bytes 2097168 | tf_op jit(solution)/shard_map/all_gather | solution.py:33
  447.5 34.1 %all-reduce.13.cloned.1.call-done = f32[256,256]{0,1:T(8,128)} async-done(((f32[256,256]{0,1:T(8,128)}), f32[256,256]{0,1:T(8,128)}) %all-reduce.13.cloned.1.call-update) | async-done | bytes 262160 | tf_op jit(solution)/shard_map/psum | solution.py:97
  483.7 11.7 %cholesky.282 = f32[128,128]{1,0:T(8,128)S(1)} custom-call(f32[128,128]{1,0:T(8,128)S(1)} %cholesky.352), custom_call_target="Cholesky" | custom-call | tf_op jit(solution)/shard_map/jit(cholesky)/cholesky | solution.py:52
  505.8 11.7 %cholesky.299 = f32[128,128]{1,0:T(8,128)S(1)} custom-call(f32[128,128]{1,0:T(8,128)S(1)} %convolution_subtract_fusion.5), custom_call_target="Cholesky" | custom-call | tf_op jit(solution)/shard_map/jit(cholesky)/cholesky | solution.py:52
  520.2 15.9 %while.10 = (s32[]{:T(128)}, f32[256,256]{1,0:T(8,128)S(1)}, s32[2,2]{1,0:T(2,128)S(1)}, f32[2,128,128]{2,1,0:T(8,128)S(1)}, s32[]{:T(128)}) while((s32[]{:T(128)}, f32[256,256]{1,0:T(8,128)S(1)}, s32[2,2]{1,0:T(2,128)S(1)}, f32[2,128,128]{2,1,0:T(8,128)S(1)}, s32[]{:T(128)}) %tuple.112), condition=%wide.while_cond.clone.1, body=%wide.while_body.clone.1.sunk | while | flops 2 | bytes 131181 | solution.py:53
  536.1 19.7 %custom-call.22 = f32[2,128,128]{1,2,0:T(8,128)S(1)} custom-call(f32[2,128,128]{2,1,0:T(8,128)S(1)} %get-tuple-element.35), custom_call_target="InvertDiagBlocksLowerTriangular" | custom-call | tf_op jit(solution)/shard_map/triangular_solve/custom-call.0 | solution.py:53
  558.1 45.1 %all-gather.11.cloned.1.call-done = f32[2048,256]{0,1:T(8,128)} async-done(((f32[512,256]{0,1:T(8,128)}), f32[2048,256]{0,1:T(8,128)}) %all-gather.11.cloned.1.call-update) | async-done | bytes 2097168 | tf_op jit(solution)/shard_map/all_gather | solution.py:33
  611.0 34.5 %all-reduce.15.cloned.1.call-done = f32[256,256]{0,1:T(8,128)} async-done(((f32[256,256]{0,1:T(8,128)}), f32[256,256]{0,1:T(8,128)}) %all-reduce.15.cloned.1.call-update) | async-done | bytes 262160 | tf_op jit(solution)/shard_map/psum | solution.py:97
  647.6 11.7 %cholesky.316 = f32[128,128]{1,0:T(8,128)S(1)} custom-call(f32[128,128]{1,0:T(8,128)S(1)} %cholesky.355), custom_call_target="Cholesky" | custom-call | tf_op jit(solution)/shard_map/jit(cholesky)/cholesky | solution.py:52
  669.7 11.7 %cholesky.333 = f32[128,128]{1,0:T(8,128)S(1)} custom-call(f32[128,128]{1,0:T(8,128)S(1)} %convolution_subtract_fusion.4), custom_call_target="Cholesky" | custom-call | tf_op jit(solution)/shard_map/jit(cholesky)/cholesky | solution.py:52
  688.3 19.9 %custom-call.24 = f32[2,128,128]{1,2,0:T(8,128)S(1)} custom-call(f32[2,128,128]{2,1,0:T(8,128)S(1)} %get-tuple-element.36), custom_call_target="InvertDiagBlocksLowerTriangular" | custom-call | tf_op jit(solution)/shard_map/triangular_solve/custom-call.0 | solution.py:53
  (147 shorter events, 134.9 us)
Async XLA Ops:
  7.4 25.3 %reduce-scatter.2.cloned.1.call-start = ((), (), s32[]{:S(2)}) async-start(), calls=%async_computation.1 | async-start | bytes 786432 | tf_op jit(solution)/shard_map/reduce_scatter | solution.py:67
  15.2 9.1 %copy-start = (s32[1,128]{1,0:T(1,128)S(1)}, s32[1,128]{1,0:T(1,128)}, u32[]{:S(2)}) copy-start(s32[1,128]{1,0:T(1,128)} %param.13) | copy-start | bytes 1540
  15.2 118.9 %all-reduce.7.cloned.1.call-start = ((), (), s32[]{:S(2)}) async-start(), calls=%async_computation.2 | async-start | bytes 8388608 | tf_op jit(solution)/shard_map/psum | solution.py:88
  52.3 81.8 %all-gather.5.cloned.1.call-start = ((), (), s32[]{:S(2)}) async-start(), calls=%async_computation.3 | async-start | bytes 2621440 | tf_op jit(solution)/shard_map/all_gather | solution.py:33
  52.9 124.8 %all-reduce.9.cloned.1.call-start = ((), (), s32[]{:S(2)}) async-start(), calls=%async_computation.4 | async-start | bytes 524288 | tf_op jit(solution)/shard_map/psum | solution.py:97
  141.9 145.3 %all-gather.7.cloned.1.call-start = ((), (), s32[]{:S(2)}) async-start(), calls=%async_computation.5 | async-start | bytes 2621440 | tf_op jit(solution)/shard_map/all_gather | solution.py:33
  242.1 87.4 %all-reduce.11.cloned.1.call-start = ((), (), s32[]{:S(2)}) async-start(), calls=%async_computation.6 | async-start | bytes 524288 | tf_op jit(solution)/shard_map/psum | solution.py:97
  295.0 144.3 %all-gather.9.cloned.1.call-start = ((), (), s32[]{:S(2)}) async-start(), calls=%async_computation.7 | async-start | bytes 2621440 | tf_op jit(solution)/shard_map/all_gather | solution.py:33
  394.2 87.4 %all-reduce.13.cloned.1.call-start = ((), (), s32[]{:S(2)}) async-start(), calls=%async_computation.8 | async-start | bytes 524288 | tf_op jit(solution)/shard_map/psum | solution.py:97
  447.2 156.0 %all-gather.11.cloned.1.call-start = ((), (), s32[]{:S(2)}) async-start(), calls=%async_computation.9 | async-start | bytes 2621440 | tf_op jit(solution)/shard_map/all_gather | solution.py:33
  558.0 87.4 %all-reduce.15.cloned.1.call-start = ((), (), s32[]{:S(2)}) async-start(), calls=%async_computation.10 | async-start | bytes 524288 | tf_op jit(solution)/shard_map/psum | solution.py:97
Sparse Core Ops, SparseCore 0:
  15.3 17.3 reduce-scatter.1
  52.4 81.6 all-reduce.6
Sparse Core Ops, SparseCore 1:
  54.3 46.3 all-gather.4
  142.0 35.6 all-reduce.8
  242.2 45.0 all-gather.6
  295.1 34.3 all-reduce.10
  394.3 45.0 all-gather.8
  447.3 34.3 all-reduce.12
  558.1 45.0 all-gather.10
  611.1 34.3 all-reduce.14
where the time goes:
time: 725 us; the launch traced here: 718 us
  waiting for transfers between devices  364 us (50%)
  other arithmetic  232 us (32%)
  matrix products  49.2 us (7%)
  blocking collectives  21.4 us (3%)
  between operations  20.9 us (3%)
  local copies, waits for them, and re-layouts  17.7 us (2%)
  loops' own time  12.9 us (2%)
    psum x4, waiting for transfers between devices, body(): gram_matrix = lax.psum(gram_of(images), 'head') / whole_basis.shape[0]  138 us
    another operation x27, other arithmetic, orthonormal(): factor = jnp.linalg.cholesky(gram_matrix)  138 us
    all_gather x4, waiting for transfers between devices, whole_of(): return lax.all_gather(basis_block, 'head', axis=0, tiled=True)  135 us
    another operation x13, other arithmetic, orthonormal(): lax.linalg.triangular_solve(factor, images, left_side=False, lower=True,...  81.6 us
    psum x1, waiting for transfers between devices, body(): covariance = lax.psum(partial_value, ('seq', 'batch')) / token_total  81.2 us
    dot_general x4, matrix products, body(): jnp.dot(covariance, whole_basis, precision=lax.Precision.HIGHEST, preferr...  24.3 us
    another operation x30, local copies, waits for them, and re-layouts, orthonormal(): lax.linalg.triangular_solve(factor, images, left_side=False, lower=True,...  16.8 us
    all_gather x1, blocking collectives, body(): lax.all_gather(joint_rows, 'head', axis=1, tiled=True)  15.5 us
  transfers between devices with their start and end apart: 10, of which 9 were waited for; matrix products, arithmetic and copies ran while one was open for 0% of the time, Pallas kernels for 0%

commit v1 on v0

--- a/solution.py
+++ b/solution.py
@@ -9,6 +9,11 @@
 ITERS = 4
 EPSILON = 1e-05
 ROTARY_BASE = 500000.0
+
+
+def by_each_axis(array, inner_axis, outer_axis):
+    inner = lax.psum(array, inner_axis)
+    return lax.psum(inner, outer_axis)
 
 
 def rotary(head_rows, position_row):
@@ -85,7 +90,7 @@
     )
     token_total = local_tokens * lax.axis_size("seq") * lax.axis_size("batch")
     basis_block = initial_basis
-    covariance = lax.psum(partial_value, ("seq", "batch")) / token_total
+    covariance = by_each_axis(partial_value, "batch", "seq") / token_total
     for iteration in range(ITERS):
         whole_basis = whole_of(basis_block)
         images = jnp.dot(

time: 725 us -> 839 us (1.16)
  waiting for transfers between devices: 364 us -> 479 us
    psum x1 -> x2, waiting for transfers between devices: 81.2 us -> 196 us  [the longest x1 110 us: by_each_axis(): return lax.psum(inner, outer_axis)]
  transfers between devices with their start and end apart: 10 -> 11, of which waited for: 9 -> 10; matrix products, arithmetic and copies ran while one was open for 0% -> 0% of each run, Pallas kernels for 0% -> 0%
where the time goes in v1:
time: 839 us; the launch traced here: 833 us
  waiting for transfers between devices  479 us (57%)
  other arithmetic  232 us (28%)
  matrix products  49.1 us (6%)
  blocking collectives  21.4 us (3%)
  between operations  20.6 us (2%)
  local copies, waits for them, and re-layouts  17.7 us (2%)
  loops' own time  12.9 us (2%)
    psum x4, waiting for transfers between devices, body(): gram_matrix = lax.psum(gram_of(images), 'head') / whole_basis.shape[0]  138 us
    another operation x27, other arithmetic, orthonormal(): factor = jnp.linalg.cholesky(gram_matrix)  138 us
    all_gather x4, waiting for transfers between devices, whole_of(): return lax.all_gather(basis_block, 'head', axis=0, tiled=True)  135 us
    psum x1, waiting for transfers between devices, by_each_axis(): return lax.psum(inner, outer_axis)  110 us
    psum x1, waiting for transfers between devices, by_each_axis(): inner = lax.psum(array, inner_axis)  85.8 us
    another operation x13, other arithmetic, orthonormal(): lax.linalg.triangular_solve(factor, images, left_side=False, lower=True,...  81.6 us
    dot_general x4, matrix products, body(): jnp.dot(covariance, whole_basis, precision=lax.Precision.HIGHEST, preferr...  24.3 us
    another operation x30, local copies, waits for them, and re-layouts, orthonormal(): lax.linalg.triangular_solve(factor, images, left_side=False, lower=True,...  16.8 us
  transfers between devices with their start and end apart: 11, of which 10 were waited for; matrix products, arithmetic and copies ran while one was open for 0% of the time, Pallas kernels for 0%

profile of v1, /device:TPU:0, one launch (start us, length us, event | category | flops | bytes accessed | tf_op | source)
XLA Modules:
  0.0 833.1 jit_solution(3968858663092362732)
XLA Ops:
  34.1 15.5 %all_gather.15 = bf16[128,2048]{0,1:T(8,128)(2,1)S(1)} all-gather(bf16[128,512]{0,1:T(8,128)(2,1)S(1)} %bitcast.160), channel_id=1, replica_groups=mesh['seq'=2,'batch'=4,'head'=4] {'head'}, dimensions={1}, use_global_device_ids=true | all-gather | bytes 655360 | tf_op jit(solution)/shard_map/all_gather | solution.py:87
  52.9 85.8 %all-reduce.8.cloned.1.call-done = f32[512,2048]{1,0:T(8,128)} async-done(((f32[512,2048]{1,0:T(8,128)}), f32[512,2048]{1,0:T(8,128)}) %all-reduce.8.cloned.1.call-update) | async-done | bytes 4194320 | tf_op jit(solution)/shard_map/psum | solution.py:15
  138.8 110.4 %all-reduce.10.cloned.1.call-done = f32[512,2048]{1,0:T(8,128)} async-done(((f32[512,2048]{1,0:T(8,128)}), f32[512,2048]{1,0:T(8,128)}) %all-reduce.10.cloned.1.call-update) | async-done | bytes 4194320 | tf_op jit(solution)/shard_map/psum | solution.py:16
  257.4 35.3 %all-reduce.12.cloned.1.call-done = f32[256,256]{0,1:T(8,128)} async-done(((f32[256,256]{0,1:T(8,128)}), f32[256,256]{0,1:T(8,128)}) %all-reduce.12.cloned.1.call-update) | async-done | bytes 262160 | tf_op jit(solution)/shard_map/psum | solution.py:102
  294.9 11.7 %cholesky.214 = f32[128,128]{1,0:T(8,128)S(1)} custom-call(f32[128,128]{1,0:T(8,128)S(1)} %cholesky.346), custom_call_target="Cholesky" | custom-call | tf_op jit(solution)/shard_map/jit(cholesky)/cholesky | solution.py:57
  306.6 9.8 %custom-call.17 = f32[1,128,128]{1,2,0:T(8,128)S(1)} custom-call(f32[1,128,128]{2,1,0:T(8,128)S(1)} %get-tuple-element.94), custom_call_target="InvertDiagBlocksLowerTriangular" | custom-call | tf_op jit(solution)/shard_map/jit(cholesky)/cholesky | solution.py:57
  316.9 11.7 %cholesky.231 = f32[128,128]{1,0:T(8,128)S(1)} custom-call(f32[128,128]{1,0:T(8,128)S(1)} %convolution_subtract_fusion.7), custom_call_target="Cholesky" | custom-call | tf_op jit(solution)/shard_map/jit(cholesky)/cholesky | solution.py:57
  335.2 19.7 %custom-call.18 = f32[2,128,128]{1,2,0:T(8,128)S(1)} custom-call(f32[2,128,128]{2,1,0:T(8,128)S(1)} %get-tuple-element.33), custom_call_target="InvertDiagBlocksLowerTriangular" | custom-call | tf_op jit(solution)/shard_map/triangular_solve/custom-call.0 | solution.py:58
  357.3 45.1 %all-gather.7.cloned.1.call-done = f32[2048,256]{0,1:T(8,128)} async-done(((f32[512,256]{0,1:T(8,128)}), f32[2048,256]{0,1:T(8,128)}) %all-gather.7.cloned.1.call-update) | async-done | bytes 2097168 | tf_op jit(solution)/shard_map/all_gather | solution.py:38
  410.4 34.3 %all-reduce.14.cloned.1.call-done = f32[256,256]{0,1:T(8,128)} async-done(((f32[256,256]{0,1:T(8,128)}), f32[256,256]{0,1:T(8,128)}) %all-reduce.14.cloned.1.call-update) | async-done | bytes 262160 | tf_op jit(solution)/shard_map/psum | solution.py:102
  446.7 11.7 %cholesky.248 = f32[128,128]{1,0:T(8,128)S(1)} custom-call(f32[128,128]{1,0:T(8,128)S(1)} %cholesky.349), custom_call_target="Cholesky" | custom-call | tf_op jit(solution)/shard_map/jit(cholesky)/cholesky | solution.py:57
  468.8 11.7 %cholesky.265 = f32[128,128]{1,0:T(8,128)S(1)} custom-call(f32[128,128]{1,0:T(8,128)S(1)} %convolution_subtract_fusion.6), custom_call_target="Cholesky" | custom-call | tf_op jit(solution)/shard_map/jit(cholesky)/cholesky | solution.py:57
  487.3 19.7 %custom-call.20 = f32[2,128,128]{1,2,0:T(8,128)S(1)} custom-call(f32[2,128,128]{2,1,0:T(8,128)S(1)} %get-tuple-element.34), custom_call_target="InvertDiagBlocksLowerTriangular" | custom-call | tf_op jit(solution)/shard_map/triangular_solve/custom-call.0 | solution.py:58
  509.4 45.1 %all-gather.9.cloned.1.call-done = f32[2048,256]{0,1:T(8,128)} async-done(((f32[512,256]{0,1:T(8,128)}), f32[2048,256]{0,1:T(8,128)}) %all-gather.9.cloned.1.call-update) | async-done | bytes 2097168 | tf_op jit(solution)/shard_map/all_gather | solution.py:38
  562.6 34.1 %all-reduce.16.cloned.1.call-done = f32[256,256]{0,1:T(8,128)} async-done(((f32[256,256]{0,1:T(8,128)}), f32[256,256]{0,1:T(8,128)}) %all-reduce.16.cloned.1.call-update) | async-done | bytes 262160 | tf_op jit(solution)/shard_map/psum | solution.py:102
  598.8 11.7 %cholesky.282 = f32[128,128]{1,0:T(8,128)S(1)} custom-call(f32[128,128]{1,0:T(8,128)S(1)} %cholesky.352), custom_call_target="Cholesky" | custom-call | tf_op jit(solution)/shard_map/jit(cholesky)/cholesky | solution.py:57
  620.9 11.7 %cholesky.299 = f32[128,128]{1,0:T(8,128)S(1)} custom-call(f32[128,128]{1,0:T(8,128)S(1)} %convolution_subtract_fusion.5), custom_call_target="Cholesky" | custom-call | tf_op jit(solution)/shard_map/jit(cholesky)/cholesky | solution.py:57
  635.3 15.9 %while.10 = (s32[]{:T(128)}, f32[256,256]{1,0:T(8,128)S(1)}, s32[2,2]{1,0:T(2,128)S(1)}, f32[2,128,128]{2,1,0:T(8,128)S(1)}, s32[]{:T(128)}) while((s32[]{:T(128)}, f32[256,256]{1,0:T(8,128)S(1)}, s32[2,2]{1,0:T(2,128)S(1)}, f32[2,128,128]{2,1,0:T(8,128)S(1)}, s32[]{:T(128)}) %tuple.114), condition=%wide.while_cond.clone.1, body=%wide.while_body.clone.1.sunk | while | flops 2 | bytes 131181 | solution.py:58
  651.2 19.7 %custom-call.22 = f32[2,128,128]{1,2,0:T(8,128)S(1)} custom-call(f32[2,128,128]{2,1,0:T(8,128)S(1)} %get-tuple-element.35), custom_call_target="InvertDiagBlocksLowerTriangular" | custom-call | tf_op jit(solution)/shard_map/triangular_solve/custom-call.0 | solution.py:58
  673.2 45.1 %all-gather.11.cloned.1.call-done = f32[2048,256]{0,1:T(8,128)} async-done(((f32[512,256]{0,1:T(8,128)}), f32[2048,256]{0,1:T(8,128)}) %all-gather.11.cloned.1.call-update) | async-done | bytes 2097168 | tf_op jit(solution)/shard_map/all_gather | solution.py:38
  726.1 34.5 %all-reduce.18.cloned.1.call-done = f32[256,256]{0,1:T(8,128)} async-done(((f32[256,256]{0,1:T(8,128)}), f32[256,256]{0,1:T(8,128)}) %all-reduce.18.cloned.1.call-update) | async-done | bytes 262160 | tf_op jit(solution)/shard_map/psum | solution.py:102
  762.7 11.7 %cholesky.316 = f32[128,128]{1,0:T(8,128)S(1)} custom-call(f32[128,128]{1,0:T(8,128)S(1)} %cholesky.355), custom_call_target="Cholesky" | custom-call | tf_op jit(solution)/shard_map/jit(cholesky)/cholesky | solution.py:57
  784.8 11.7 %cholesky.333 = f32[128,128]{1,0:T(8,128)S(1)} custom-call(f32[128,128]{1,0:T(8,128)S(1)} %convolution_subtract_fusion.4), custom_call_target="Cholesky" | custom-call | tf_op jit(solution)/shard_map/jit(cholesky)/cholesky | solution.py:57
  803.4 19.9 %custom-call.24 = f32[2,128,128]{1,2,0:T(8,128)S(1)} custom-call(f32[2,128,128]{2,1,0:T(8,128)S(1)} %get-tuple-element.36), custom_call_target="InvertDiagBlocksLowerTriangular" | custom-call | tf_op jit(solution)/shard_map/triangular_solve/custom-call.0 | solution.py:58
  (150 shorter events, 144.7 us)
Async XLA Ops:
  7.4 25.3 %reduce-scatter.2.cloned.1.call-start = ((), (), s32[]{:S(2)}) async-start(), calls=%async_computation.1 | async-start | bytes 786432 | tf_op jit(solution)/shard_map/reduce_scatter | solution.py:72
  15.2 9.1 %copy-start = (s32[1,128]{1,0:T(1,128)S(1)}, s32[1,128]{1,0:T(1,128)}, u32[]{:S(2)}) copy-start(s32[1,128]{1,0:T(1,128)} %param.13) | copy-start | bytes 1540
  15.2 123.5 %all-reduce.8.cloned.1.call-start = ((), (), s32[]{:S(2)}) async-start(), calls=%async_computation.2 | async-start | bytes 8388608 | tf_op jit(solution)/shard_map/psum | solution.py:15
  52.2 86.6 %all-gather.5.cloned.1.call-start = ((), (), s32[]{:S(2)}) async-start(), calls=%async_computation.4 | async-start | bytes 2621440 | tf_op jit(solution)/shard_map/all_gather | solution.py:38
  52.8 196.4 %all-reduce.10.cloned.1.call-start = ((), (), s32[]{:S(2)}) async-start(), calls=%async_computation.3 | async-start | bytes 8388608 | tf_op jit(solution)/shard_map/psum | solution.py:16
  138.7 154.0 %all-reduce.12.cloned.1.call-start = ((), (), s32[]{:S(2)}) async-start(), calls=%async_computation.5 | async-start | bytes 524288 | tf_op jit(solution)/shard_map/psum | solution.py:102
  257.1 145.3 %all-gather.7.cloned.1.call-start = ((), (), s32[]{:S(2)}) async-start(), calls=%async_computation.6 | async-start | bytes 2621440 | tf_op jit(solution)/shard_map/all_gather | solution.py:38
  357.2 87.4 %all-reduce.14.cloned.1.call-start = ((), (), s32[]{:S(2)}) async-start(), calls=%async_computation.7 | async-start | bytes 524288 | tf_op jit(solution)/shard_map/psum | solution.py:102
  410.1 144.3 %all-gather.9.cloned.1.call-start = ((), (), s32[]{:S(2)}) async-start(), calls=%async_computation.8 | async-start | bytes 2621440 | tf_op jit(solution)/shard_map/all_gather | solution.py:38
  509.3 87.4 %all-reduce.16.cloned.1.call-start = ((), (), s32[]{:S(2)}) async-start(), calls=%async_computation.9 | async-start | bytes 524288 | tf_op jit(solution)/shard_map/psum | solution.py:102
  562.3 156.0 %all-gather.11.cloned.1.call-start = ((), (), s32[]{:S(2)}) async-start(), calls=%async_computation.10 | async-start | bytes 2621440 | tf_op jit(solution)/shard_map/all_gather | solution.py:38
  673.1 87.4 %all-reduce.18.cloned.1.call-start = ((), (), s32[]{:S(2)}) async-start(), calls=%async_computation.11 | async-start | bytes 524288 | tf_op jit(solution)/shard_map/psum | solution.py:102
Sparse Core Ops, SparseCore 0:
  15.3 17.3 reduce-scatter.1
  52.4 86.2 all-reduce.7
  141.1 108.0 all-reduce.9
Sparse Core Ops, SparseCore 1:
  54.3 46.3 all-gather.4
  257.2 35.5 all-reduce.11
  357.3 45.0 all-gather.6
  410.2 34.3 all-reduce.13
  509.4 45.0 all-gather.8
  562.3 34.3 all-reduce.15
  673.2 45.0 all-gather.10
  726.2 34.3 all-reduce.17
